TPU v7x, 32 devices: a whole 2x2x4 slice. The times are simulated.
32 devices in a mesh: pipe: 4 (over y, x), ctx: 2 (over core), tp: 4 (over z).
Axes of the slice: x: 2, y: 2, z: 4, core: 2. Of those that a mesh axis runs over, the one named last changes fastest.
Arguments:
- mamba_input: bfloat16 [4, 768, 8192], P('pipe', 'ctx', 'tp'), may hold values from -6 to 6
- mamba_bc: bfloat16 [4, 768, 2, 512], P('pipe', 'ctx', None, 'tp'), may hold values from -6 to 6
- gate_input: bfloat16 [4, 768, 8192], P('pipe', 'ctx', 'tp'), may hold values from -6 to 6
- step_input: bfloat16 [4, 768, 128], P('pipe', 'ctx', 'tp'), may hold values from -4 to 4
- step_bias: float32 [4, 128], P('pipe', 'tp'), may hold values from -1 to 1
- decay_rate: float32 [4, 128], P('pipe', 'tp'), may hold values from 6.510417e-05 to 0.03
- skip_gain: float32 [4, 128], P('pipe', 'tp'), may hold values from 0.5 to 1.5
- conv_weight: float32 [4, 4, 8192], P('pipe', None, 'tp'), may hold values from -3 to 3
- conv_bc_weight: float32 [4, 4, 2, 512], P('pipe', None, None, 'tp'), may hold values from -3 to 3
- norm_gain: float32 [4, 8192], P('pipe', 'tp'), may hold values from 0.5 to 1.5
- queries: bfloat16 [4, 768, 4096], P('pipe', 'ctx', 'tp'), may hold values from -160 to 160
- attn_keys: bfloat16 [4, 768, 512], P('pipe', 'ctx', 'tp'), may hold values from -7 to 7
- attn_values: bfloat16 [4, 768, 512], P('pipe', 'ctx', 'tp'), may hold values from -6 to 6
- documents: int32 [4, 768], P('pipe'), may hold values from 0 to 3, never falling along the last dimension, each value on 1 to 384 neighbouring positions
Outputs:
- mixer_out: bfloat16 [4, 768, 8192], P('pipe', 'ctx', 'tp')
- attn_out: bfloat16 [4, 768, 4096], P('pipe', 'ctx', 'tp')
All inputs are finite; a program needn't handle non-finite values.
Results may differ from a plain program's by a relative error of at most 0.0035.
Values may be sent and summed in bfloat16 or wider, within the bound.
A program may use at most 64 MiB of HBM per device.

v0:
```python
import math

import jax
import jax.numpy as jnp
from jax import lax
from jax.sharding import PartitionSpec as P

HDIM = 64
STATE = 128
KERNEL = 4
ADIM = 128


highest = lax.Precision.HIGHEST


def shifted(value, axis, by):
    devices = lax.axis_size(axis)
    pairs = [(i, i + by) for i in range(devices) if 0 <= i + by < devices]
    return lax.ppermute(value, axis, pairs)


def shifted_2(value, axis, steps):
    count = lax.axis_size(axis)
    pairs = [(source, (source + steps) % count) for source in range(count)]
    return lax.ppermute(value, axis, pairs)


def conv_silu(padded, weight, length):
    summed = jnp.zeros((length,) + padded.shape[1:], jnp.float32)
    for offset in range(weight.shape[0]):
        summed = summed + weight[offset] * padded[offset : offset + length].astype(jnp.float32)
    return jax.nn.silu(summed)


def local_scan(x_block, b_block, c_block, step_block, log_block, groups):
    length, head_count, head_size = x_block.shape
    per_group = head_count // groups
    cumulative = jnp.cumsum(log_block, axis=0)
    gram_matrix = jnp.einsum("tgn,sgn->gts", c_block, b_block, precision=highest)
    spread = cumulative.T[:, :, None] - cumulative.T[:, None, :]
    row_index = lax.broadcasted_iota(jnp.int32, (length, length), 0)
    col_index = lax.broadcasted_iota(jnp.int32, (length, length), 1)
    decays = jnp.exp(jnp.where(row_index >= col_index, spread, -jnp.inf))
    weights = (
        decays.reshape(groups, per_group, length, length)
        * gram_matrix[:, None]
        * step_block.T.reshape(groups, per_group, 1, length)
    )
    inside = jnp.einsum(
        "ghts,sghp->tghp",
        weights,
        x_block.reshape(length, groups, per_group, head_size),
        precision=highest,
    )
    inside = inside.reshape(length, head_count, head_size)
    end_log = cumulative[-1]
    tail_decay = jnp.exp(end_log[None, :] - cumulative) * step_block
    weighted = (x_block * tail_decay[:, :, None]).reshape(length, groups, per_group, head_size)
    contrib = jnp.einsum("tgn,tghp->ghpn", b_block, weighted, precision=highest).reshape(
        head_count, head_size, -1
    )
    return (inside, contrib, jnp.exp(end_log), cumulative)


def incoming_term(c_block, carried, cumulative, groups):
    length, head_count = cumulative.shape
    head_size = carried.shape[1]
    per_group = head_count // groups
    grid = carried.reshape(groups, per_group, head_size, -1)
    result = jnp.einsum("tgn,ghpn->tghp", c_block, grid, precision=highest).reshape(
        length, head_count, head_size
    )
    return result * jnp.exp(cumulative)[:, :, None]


def gated_norm(ssd_out, gate_in, gain_in, groups):
    gated_out = ssd_out * jax.nn.silu(gate_in.astype(jnp.float32))
    row_count, width = gated_out.shape
    grouped = gated_out.reshape(row_count, groups, width // groups)
    mean_square = jnp.mean(grouped * grouped, axis=-1, keepdims=True)
    normed = (grouped * lax.rsqrt(mean_square + 1e-05)).reshape(row_count, width)
    return (normed * gain_in).astype(jnp.bfloat16)


def attend_block(
    carry, query_tile_layout, query_pos, query_doc, doc_all, key_block, value_block, block_start
):
    row_max, row_sum_running, accum = carry
    span = key_block.shape[0]
    kv_count = query_tile_layout.shape[1]
    key_tile_layout = key_block.reshape(span, kv_count, ADIM)
    value_grid = value_block.reshape(span, kv_count, ADIM)
    attention_logits = jnp.einsum(
        "hbau,zbu->bahz", query_tile_layout, key_tile_layout, preferred_element_type=jnp.float32
    ) * (1.0 / math.sqrt(ADIM))
    key_pos = block_start + jnp.arange(span, dtype=jnp.int32)
    key_doc = lax.dynamic_slice_in_dim(doc_all, block_start, span)
    allowed = (key_pos[None, :] <= query_pos[:, None]) & (key_doc[None, :] == query_doc[:, None])
    masked = jnp.where(allowed, attention_logits, -1e30)
    new_max = jnp.maximum(row_max, jnp.max(masked, axis=-1))
    rescale = jnp.exp(row_max - new_max)
    weights_exp = jnp.where(allowed, jnp.exp(masked - new_max[..., None]), 0.0)
    new_total = row_sum_running * rescale + jnp.sum(weights_exp, axis=-1)
    product = jnp.einsum(
        "ljnx,xlc->ljnc",
        weights_exp.astype(jnp.bfloat16),
        value_grid,
        preferred_element_type=jnp.float32,
    )
    return (new_max, new_total, accum * rescale[..., None] + product)


def fold_keys(carry, query_tile_layout, query_pos, query_doc, doc_all, pieces, block_rows):
    key_piece, value_piece = pieces
    span = key_piece.shape[0]

    def over_blocks(inner_carry, block_number):
        offset_rows = block_number * block_rows
        key_block = lax.dynamic_slice_in_dim(key_piece, offset_rows, block_rows)
        value_block = lax.dynamic_slice_in_dim(value_piece, offset_rows, block_rows)
        return (
            attend_block(
                inner_carry,
                query_tile_layout,
                query_pos,
                query_doc,
                doc_all,
                key_block,
                value_block,
                offset_rows,
            ),
            None,
        )

    result, unused = lax.scan(over_blocks, carry, jnp.arange(span // block_rows, dtype=jnp.int32))
    return result


def start_state(kv_count, per_kv, rows):
    return (
        jnp.full((kv_count, per_kv, rows), -1e30, jnp.float32),
        jnp.zeros((kv_count, per_kv, rows), jnp.float32),
        jnp.zeros((kv_count, per_kv, rows, ADIM), jnp.float32),
    )


def finish_rows(carry):
    row_max, row_sum_running, accum = carry
    rows = accum.shape[2]
    return (
        (accum / row_sum_running[..., None])
        .transpose(2, 0, 1, 3)
        .reshape(rows, -1)
        .astype(jnp.bfloat16)
    )


def local(
    mamba_input,
    mamba_bc,
    gate_input,
    step_input,
    step_bias,
    decay_rate,
    skip_gain,
    conv_weight,
    conv_bc_weight,
    norm_gain,
    queries,
    attn_keys,
    attn_values,
    documents,
):
    x_local = mamba_input[0]
    bc_local = mamba_bc[0]
    row_count = x_local.shape[0]
    margin = KERNEL - 1
    tail_x, tail_bc = shifted(
        (x_local[row_count - margin :], bc_local[row_count - margin :]), "ctx", 1
    )
    x_conv = conv_silu(jnp.concatenate([tail_x, x_local], 0), conv_weight[0], row_count)
    bc_conv = conv_silu(jnp.concatenate([tail_bc, bc_local], 0), conv_bc_weight[0], row_count)
    head_count = step_input.shape[-1]
    group_count = bc_local.shape[-1] // STATE
    x_heads = x_conv.reshape(row_count, head_count, HDIM)
    b_groups = bc_conv[:, 0].reshape(row_count, group_count, STATE)
    c_groups = bc_conv[:, 1].reshape(row_count, group_count, STATE)
    step_size = jax.nn.softplus(step_input[0].astype(jnp.float32) + step_bias[0])
    log_decay = -decay_rate[0] * step_size
    inside, contrib, shard_decay, cumulative = local_scan(
        x_heads, b_groups, c_groups, step_size, log_decay, group_count
    )

    def chain_step(hop_index, received):
        return shifted(
            (shard_decay[:, None, None] * received + contrib).astype(jnp.bfloat16), "ctx", 1
        ).astype(jnp.float32)

    carried = lax.fori_loop(0, lax.axis_size("ctx") - 1, chain_step, jnp.zeros_like(contrib))
    incoming_part = incoming_term(c_groups, carried, cumulative, group_count)
    ssd_out = (inside + incoming_part + skip_gain[0][None, :, None] * x_heads).reshape(
        row_count, -1
    )
    mixer_result = gated_norm(ssd_out, gate_input[0], norm_gain[0], group_count)
    query_local = queries[0]
    key_local = attn_keys[0]
    value_local = attn_values[0]
    doc_all = documents[0]
    kv_count = key_local.shape[1] // ADIM
    per_kv = query_local.shape[1] // ADIM // kv_count
    first_row = lax.axis_index("ctx") * row_count
    query_tile_layout = query_local.reshape(row_count, kv_count, per_kv, ADIM)
    query_pos = first_row + jnp.arange(row_count, dtype=jnp.int32)
    query_doc = lax.dynamic_slice_in_dim(doc_all, first_row, row_count)
    initial = start_state(kv_count, per_kv, row_count)
    final_state = fold_keys(
        initial,
        query_tile_layout,
        query_pos,
        query_doc,
        doc_all,
        (
            lax.all_gather(key_local, "ctx", axis=0, tiled=True),
            lax.all_gather(value_local, "ctx", axis=0, tiled=True),
        ),
        row_count,
    )
    attended = finish_rows(final_state)
    passed_mix, passed_attn = shifted_2((mixer_result, attended), "pipe", 1)
    return (passed_mix[None], passed_attn[None])


def solution(mesh):
    in_specs = (
        P("pipe", "ctx", "tp"),
        P("pipe", "ctx", None, "tp"),
        P("pipe", "ctx", "tp"),
        P("pipe", "ctx", "tp"),
        P("pipe", "tp"),
        P("pipe", "tp"),
        P("pipe", "tp"),
        P("pipe", None, "tp"),
        P("pipe", None, None, "tp"),
        P("pipe", "tp"),
        P("pipe", "ctx", "tp"),
        P("pipe", "ctx", "tp"),
        P("pipe", "ctx", "tp"),
        P("pipe", None),
    )
    out_specs = (P("pipe", "ctx", "tp"), P("pipe", "ctx", "tp"))
    return jax.shard_map(local, mesh=mesh, in_specs=in_specs, out_specs=out_specs, check_vma=False)
```

profile of v0, /device:TPU:1, one launch (start us, length us, event | category | flops | bytes accessed | tf_op | source)
XLA Modules:
  0.0 118.3 jit_solution(10643560121616881138)
XLA Ops:
  0.7 2.0 %copy.27 = bf16[1,384,2048]{1,2,0:T(8,128)(2,1)S(1)} copy(bf16[1,384,2048]{2,1,0:T(8,128)(2,1)} %param.16) | data formatting | bytes 3145728 | tf_op args[0]
  2.8 1.0 slice_bitcast_fusion
  3.8 1.3 %collective-permute-start = (bf16[3,2048]{0,1:T(8,128)(2,1)}, bf16[3,2048]{0,1:T(8,128)(2,1)}, u32[]{:S(2)}, u32[]{:S(2)}) collective-permute-start(bf16[3,2048]{0,1:T(8,128)(2,1)} %slice_bitcast_fusion), channel_id=1, source_target_pairs={{0,4},{1,5},{2,6},{3,7},{8,12},{9,13},{10,14},{11,15},{16,20},{17,... | collective-permute-start | bytes 36872 | tf_op jit(solution)/shard_map/ppermute | solution.py:20
  5.1 0.6 slice_bitcast_fusion.1
  5.7 1.3 %collective-permute-start.1 = (bf16[3,2,128]{2,0,1:T(4,128)(2,1)}, bf16[3,2,128]{2,0,1:T(4,128)(2,1)}, u32[]{:S(2)}, u32[]{:S(2)}) collective-permute-start(bf16[3,2,128]{2,0,1:T(4,128)(2,1)} %slice_bitcast_fusion.1), channel_id=1, source_target_pairs={{0,4},{1,5},{2,6},{3,7},{8,12},{9,13},{10,14},{11,15},{16,20},{17,... | collective-permute-start | bytes 4616 | tf_op jit(solution)/shard_map/ppermute | solution.py:20
  7.0 0.7 iota_compare_fusion
  7.8 0.9 reduce-window.6
  8.7 0.2 slice_reduce_fusion
  8.9 0.7 copy_bitcast_fusion.1
  9.6 0.2 slice_reduce_fusion.1
  9.8 0.8 bitcast_exponential_fusion
  10.6 0.5 exponential_multiply_fusion.1
  11.1 0.6 fusion.68
  11.7 0.6 slice_bitcast_fusion.5
  12.3 4.1 %all-gather = bf16[1,768,128]{2,1,0:T(8,128)(2,1)S(1)} all-gather(bf16[1,384,128]{2,1,0:T(8,128)(2,1)S(1)} %copy-done.9), channel_id=2, replica_groups=mesh['pipe'=4,'ctx'=2,'tp'=4] {'ctx'}, dimensions={1}, use_global_device_ids=true | all-gather | bytes 294912 | tf_op jit(solution)/shard_map/all_gather | solution.py:224
  16.4 2.1 %all-gather.1 = bf16[1,768,128]{2,1,0:T(8,128)(2,1)} all-gather(bf16[1,384,128]{2,1,0:T(8,128)(2,1)S(1)} %copy-done.10), channel_id=3, replica_groups=mesh['pipe'=4,'ctx'=2,'tp'=4] {'ctx'}, dimensions={1}, use_global_device_ids=true | all-gather | bytes 294912 | tf_op jit(solution)/shard_map/all_gather | solution.py:225
  18.5 2.6 %copy.33 = bf16[1,384,2048]{1,2,0:T(8,128)(2,1)} copy(bf16[1,384,2048]{2,1,0:T(8,128)(2,1)} %param.18) | data formatting | bytes 3145728 | tf_op args[2]
  21.1 0.7 mul.282
  21.8 0.4 copy.34
  22.2 0.4 copy.35
  22.6 1.1 divide_multiply_fusion.1
  23.7 0.6 fusion.50
  24.4 5.1 %bitcast_multiply_fusion.1 = (f32[384,2048]{0,1:T(8,128)S(1)}, f32[384,2048]{0,1:T(8,128)S(1)}) fusion(f32[384,32]{0,1:T(8,128)} %get-tuple-element.163, bf16[384,2048]{0,1:T(8,128)(2,1)S(1)} %bitcast.191, f32[2048]{0:T(1024)} %bitcast.205, bf16[3,2048]{0,1:T(8,128)(2,1)} %collective-permute-done, f32[2048]{0:T(1024)} %bitcast.206, f32[2048]{0:T(1024)} %bitcast.204, ...), kind=kLoop, calls=%fused_computation.51 | loop fusion | flops 19660800 | bytes 7958528 | tf_op jit(solution)/shard_map/mul | solution.py:59
  29.6 2.7 %fusion.43 = bf16[32,64,128]{2,1,0:T(8,128)(2,1)S(1)} fusion(f32[384,32,64]{0,2,1:T(8,128)S(1)} %bitcast.189, f32[32]{0:T(128)S(1)} %copy-done.19, f32[384,2,128]{2,0,1:T(8,128)S(1)} %divide_multiply_fusion.1), kind=kOutput, calls=%fused_computation.64 | convolution fusion | flops 1208483840 | bytes 3867136 | tf_op jit(solution)/shard_map/tgn,tghp->ghpn/dot_general | solution.py:60
  32.3 1.5 %collective-permute-start.2 = (bf16[32,64,128]{2,1,0:T(8,128)(2,1)S(1)}, bf16[32,64,128]{2,1,0:T(8,128)(2,1)S(1)}, u32[]{:S(2)}, u32[]{:S(2)}) collective-permute-start(bf16[32,64,128]{2,1,0:T(8,128)(2,1)S(1)} %fusion.43), channel_id=1, source_target_pairs={{0,4},{1,5},{2,6},{3,7},{8,12},{9,13},{10,14},{11,15},{16,20},{17,... | collective-permute-start | bytes 1572872 | tf_op jit(solution)/shard_map/while/body/eval_jaxpr/ppermute | solution.py:20
  33.8 23.1 %fusion.23 = f32[32,64,384]{2,1,0:T(8,128)S(1)} fusion(f32[384,32,64]{0,2,1:T(8,128)S(1)} %bitcast.190, f32[32,384]{1,0:T(8,128)S(1)} %copy-done.11, f32[384,384]{1,0:T(8,128)S(1)} %fusion.50, f32[32,384]{1,0:T(8,128)S(1)} %copy-done.12, pred[384,384]{1,0:T(8,128)(4,1)S(1)} %copy-done.7), kind=kOutput, calls=%fused_computation.30 | convolution fusion | flops 3642753024 | bytes 7127040 | tf_op jit(solution)/shard_map/ghts,sghp->tghp/dot_general | solution.py:50
  57.0 1.5 %fusion.47 = f32[32,64,384]{2,1,0:T(8,128)S(1)} fusion(bf16[32,64,128]{2,1,0:T(8,128)(2,1)S(1)} %collective-permute-done.2, f32[384,2,128]{2,0,1:T(8,128)S(1)} %divide_multiply_fusion.1), kind=kOutput, calls=%fused_computation.75 | convolution fusion | flops 1207959552 | bytes 3866624 | tf_op jit(solution)/shard_map/tgn,ghpn->tghp/dot_general | solution.py:71
  58.5 2.1 %multiply_reduce_fusion = (f32[384]{0:T(512)S(1)}, f32[384,2048]{0,1:T(8,128)S(1)}) fusion(bf16[1,384,2048]{1,2,0:T(8,128)(2,1)S(1)} %copy-done.1, f32[384,2048]{0,1:T(8,128)S(1)} %get-tuple-element.153, f32[2048]{0:T(1024)S(1)} %copy-done.13, f32[384,32]{0,1:T(8,128)S(1)} %copy-done.6, f32[32,64,384]{2,1,0:T(8,128)S(1)} %fusion.47, ...), kind=kLoop, calls=%fused_computation.53 | loop fusion | flops 9436800 | bytes 14214656 | tf_op jit(solution)/shard_map/reduce_sum | solution.py:81
  60.7 1.5 %multiply_convert_fusion = bf16[384,2048]{0,1:T(8,128)(2,1)} fusion(f32[384,2048]{0,1:T(8,128)S(1)} %get-tuple-element.151, f32[2048]{0:T(1024)S(1)} %bitcast.209, f32[384]{0:T(512)S(1)} %add_rsqrt_fusion), kind=kLoop, calls=%fused_computation.52 | loop fusion | flops 2359296 | bytes 4728320 | tf_op jit(solution)/shard_map/convert_element_type | solution.py:83
  62.2 2.0 %collective-permute-start.3 = (bf16[384,2048]{0,1:T(8,128)(2,1)}, bf16[384,2048]{0,1:T(8,128)(2,1)S(1)}, u32[]{:S(2)}, u32[]{:S(2)}) collective-permute-start(bf16[384,2048]{0,1:T(8,128)(2,1)} %multiply_convert_fusion), channel_id=1, source_target_pairs={{0,8},{8,16},{16,24},{24,0},{1,9},{9,17},{17,25},{25,1},{2,10},{10... | collective-permute-start | bytes 4718600 | tf_op jit(solution)/shard_map/ppermute | solution.py:26
  64.2 22.5 %while.5 = (s32[]{:T(128)}, f32[1,8,384]{2,1,0:T(8,128)S(1)}, f32[1,8,384]{2,1,0:T(8,128)S(1)}, f32[1,8,384,128]{3,2,1,0:T(8,128)}, s32[2]{0:T(128)S(1)}, /*inde...) while((s32[]{:T(128)}, f32[1,8,384]{2,1,0:T(8,128)S(1)}, ...), condition=%wide.region_6.7_spmd.clone, body=%wide.region_3.6_spmd.clone.sunk | while | flops 620956416 | bytes 37957888 | solution.py:136
  64.2 0.6 dynamic_slice.41
  65.5 0.2 compare_and_fusion.2
  65.7 3.0 %fusion.79 = (f32[8,384]{1,0:T(8,128)S(1)}, f32[384,384,8]{1,0,2:T(8,128)}) fusion(pred[384,384]{0,1:T(8,128)(4,1)S(1)} %compare_and_fusion.2, bf16[384,1,8,128]{3,0,2,1:T(8,128)(2,1)S(1)} %get-tuple-element.290, bf16[768,128]{1,0:T(8,128)(2,1)S(1)} %get-tuple-element.289, s32[]{:T(128)S(6)} %select_n.78), kind=kOutput, calls=%fused_computation.3.clone.1 | convolution fusion | flops 305525760 | bytes 5763076 | tf_op jit(solution)/shard_map/while/body/eval_jaxpr/hbau,zbu->bahz/dot_general | solution.py:94
  68.8 5.3 %bitcast_add_fusion.5 = f32[1,8,384,128]{3,2,1,0:T(8,128)} fusion(f32[1,8,384,128]{3,2,1,0:T(8,128)} %get-tuple-element.270, f32[384,384,8]{1,0,2:T(8,128)} %get-tuple-element.250, f32[8,384]{1,0:T(8,128)S(1)} %bitcast.192, pred[384,384]{0,1:T(8,128)(4,1)S(1)} %compare_and_fusion.2, f32[8,384]{1,0:T(8,128)S(1)} %get-tuple-element.251, ...), kind=kOutput, calls=%fused_computation.9.clone.1 | convolution fusion | flops 309067776 | bytes 8134661 | tf_op jit(solution)/shard_map/while/body/eval_jaxpr/ljnx,xlc->ljnc/dot_general | solution.py:105
  74.0 1.1 fusion.81
  75.2 0.6 dynamic_slice.41
  76.6 0.2 compare_and_fusion.2
  76.8 3.0 %fusion.79 = (f32[8,384]{1,0:T(8,128)S(1)}, f32[384,384,8]{1,0,2:T(8,128)}) fusion(pred[384,384]{0,1:T(8,128)(4,1)S(1)} %compare_and_fusion.2, bf16[384,1,8,128]{3,0,2,1:T(8,128)(2,1)S(1)} %get-tuple-element.290, bf16[768,128]{1,0:T(8,128)(2,1)S(1)} %get-tuple-element.289, s32[]{:T(128)S(6)} %select_n.78), kind=kOutput, calls=%fused_computation.3.clone.1 | convolution fusion | flops 305525760 | bytes 5763076 | tf_op jit(solution)/shard_map/while/body/eval_jaxpr/hbau,zbu->bahz/dot_general | solution.py:94
  79.8 5.8 %bitcast_add_fusion.5 = f32[1,8,384,128]{3,2,1,0:T(8,128)} fusion(f32[1,8,384,128]{3,2,1,0:T(8,128)} %get-tuple-element.270, f32[384,384,8]{1,0,2:T(8,128)} %get-tuple-element.250, f32[8,384]{1,0:T(8,128)S(1)} %bitcast.192, pred[384,384]{0,1:T(8,128)(4,1)S(1)} %compare_and_fusion.2, f32[8,384]{1,0:T(8,128)S(1)} %get-tuple-element.251, ...), kind=kOutput, calls=%fused_computation.9.clone.1 | convolution fusion | flops 309067776 | bytes 8134661 | tf_op jit(solution)/shard_map/while/body/eval_jaxpr/ljnx,xlc->ljnc/dot_general | solution.py:105
  85.6 1.1 fusion.81
  86.8 1.9 %fusion.44 = bf16[384,1,8,128]{3,0,2,1:T(8,128)(2,1)S(1)} fusion(f32[1,8,384,128]{3,2,1,0:T(8,128)} %get-tuple-element.72, f32[8,384]{1,0:T(8,128)S(1)} %bitcast.201), kind=kLoop, calls=%fused_computation.66 | loop fusion | flops 786432 | bytes 2371584 | tf_op jit(solution)/shard_map/convert_element_type | solution.py:155
  88.7 0.5 copy.36
  89.2 0.2 copy.53
  89.4 1.3 %collective-permute-start.4 = (bf16[384,1024]{1,0:T(8,128)(2,1)S(1)}, bf16[384,1024]{1,0:T(8,128)(2,1)S(1)}, u32[]{:S(2)}, u32[]{:S(2)}) collective-permute-start(bf16[384,1024]{1,0:T(8,128)(2,1)S(1)} %bitcast.200), channel_id=1, source_target_pairs={{0,8},{8,16},{16,24},{24,0},{1,9},{9,17},{17,25},{25,1},{2,10},{10... | collective-permute-start | bytes 2359304 | tf_op jit(solution)/shard_map/ppermute | solution.py:26
  90.6 25.2 %collective-permute-done.4 = bf16[384,1024]{1,0:T(8,128)(2,1)S(1)} collective-permute-done((bf16[384,1024]{1,0:T(8,128)(2,1)S(1)}, bf16[384,1024]{1,0:T(8,128)(2,1)S(1)}, u32[]{:S(2)}, u32[]{:S(2)}) %collective-permute-start.4) | collective-permute-done | bytes 786464 | tf_op jit(solution)/shard_map/ppermute | solution.py:26
  115.8 1.6 %copy.37 = bf16[1,384,2048]{2,1,0:T(8,128)(2,1)} copy(bf16[1,384,2048]{1,2,0:T(8,128)(2,1)S(1)} %bitcast.197) | data formatting | bytes 3145728
  117.4 0.9 copy.68
  (72 shorter events, 0.6 us)
Async XLA Ops:
  0.6 4.4 %copy-start.4 = (bf16[1,384,2,128]{3,2,1,0:T(2,128)(2,1)S(1)}, bf16[1,384,2,128]{3,2,1,0:T(2,128)(2,1)}, u32[]{:S(2)}) copy-start(bf16[1,384,2,128]{3,2,1,0:T(2,128)(2,1)} %param.17) | copy-start | bytes 589828
  0.6 7.1 %copy-start.21 = (f32[1,32]{1,0:T(1,128)S(1)}, f32[1,32]{1,0:T(1,128)}, u32[]{:S(2)}) copy-start(f32[1,32]{1,0:T(1,128)} %param.21) | copy-start | bytes 388
  0.7 7.0 %copy-start.18 = (f32[1,32]{1,0:T(1,128)S(1)}, f32[1,32]{1,0:T(1,128)}, u32[]{:S(2)}) copy-start(f32[1,32]{1,0:T(1,128)} %param.20) | copy-start | bytes 388
  0.7 7.0 %copy-start.8 = (bf16[1,384,32]{1,2,0:T(8,128)(2,1)S(1)}, bf16[1,384,32]{1,2,0:T(8,128)(2,1)}, u32[]{:S(2)}) copy-start(bf16[1,384,32]{1,2,0:T(8,128)(2,1)} %param.19) | copy-start | bytes 73732
  0.7 10.4 %copy-start.14 = (f32[1,4,2048]{2,1,0:T(4,128)S(1)}, f32[1,4,2048]{2,1,0:T(4,128)}, u32[]{:S(2)}) copy-start(f32[1,4,2048]{2,1,0:T(4,128)} %param.23) | copy-start | bytes 98308
  0.7 11.1 %copy-start.17 = (f32[1,4,2,128]{3,2,1,0:T(2,128)S(1)}, f32[1,4,2,128]{3,2,1,0:T(2,128)}, u32[]{:S(2)}) copy-start(f32[1,4,2,128]{3,2,1,0:T(2,128)} %param.24) | copy-start | bytes 12292
  0.7 11.7 %copy-start.9 = (bf16[1,384,128]{2,1,0:T(8,128)(2,1)S(1)}, bf16[1,384,128]{2,1,0:T(8,128)(2,1)}, u32[]{:S(2)}) copy-start(bf16[1,384,128]{2,1,0:T(8,128)(2,1)} %param.27) | copy-start | bytes 294916
  0.7 15.7 %copy-start.10 = (bf16[1,384,128]{2,1,0:T(8,128)(2,1)S(1)}, bf16[1,384,128]{2,1,0:T(8,128)(2,1)}, u32[]{:S(2)}) copy-start(bf16[1,384,128]{2,1,0:T(8,128)(2,1)} %param.28) | copy-start | bytes 294916
  2.7 18.3 %copy-start.20 = (f32[1,32]{1,0:T(1,128)S(1)}, f32[1,32]{1,0:T(1,128)}, u32[]{:S(2)}) copy-start(f32[1,32]{1,0:T(1,128)} %param.22) | copy-start | bytes 388
  2.8 19.1 %copy-start.2 = (bf16[1,384,1024]{2,1,0:T(8,128)(2,1)S(1)}, bf16[1,384,1024]{2,1,0:T(8,128)(2,1)}, u32[]{:S(2)}) copy-start(bf16[1,384,1024]{2,1,0:T(8,128)(2,1)} %param.26) | copy-start | bytes 2359300
  3.8 20.6 %collective-permute-start = (bf16[3,2048]{0,1:T(8,128)(2,1)}, bf16[3,2048]{0,1:T(8,128)(2,1)}, u32[]{:S(2)}, u32[]{:S(2)}) collective-permute-start(bf16[3,2048]{0,1:T(8,128)(2,1)} %slice_bitcast_fusion), channel_id=1, source_target_pairs={{0,4},{1,5},{2,6},{3,7},{8,12},{9,13},{10,14},{11,15},{16,20},{17,... | collective-permute-start | bytes 36872 | tf_op jit(solution)/shard_map/ppermute | solution.py:20
  5.7 16.9 %collective-permute-start.1 = (bf16[3,2,128]{2,0,1:T(4,128)(2,1)}, bf16[3,2,128]{2,0,1:T(4,128)(2,1)}, u32[]{:S(2)}, u32[]{:S(2)}) collective-permute-start(bf16[3,2,128]{2,0,1:T(4,128)(2,1)} %slice_bitcast_fusion.1), channel_id=1, source_target_pairs={{0,4},{1,5},{2,6},{3,7},{8,12},{9,13},{10,14},{11,15},{16,20},{17,... | collective-permute-start | bytes 4616 | tf_op jit(solution)/shard_map/ppermute | solution.py:20
  18.5 4.1 %copy-start.16 = (s32[1,768]{1,0:T(1,128)S(1)}, s32[1,768]{1,0:T(1,128)}, u32[]{:S(2)}) copy-start(s32[1,768]{1,0:T(1,128)} %param.29) | copy-start | bytes 9220
  24.4 5.2 %copy-start.19 = (f32[32]{0:T(128)S(1)}, f32[32]{0:T(128)}, u32[]{:S(2)}) copy-start(f32[32]{0:T(128)} %exponential_multiply_fusion.1) | copy-start | bytes 388
  29.5 4.3 %copy-start.7 = (pred[384,384]{1,0:T(8,128)(4,1)S(1)}, pred[384,384]{1,0:T(8,128)(4,1)}, u32[]{:S(2)}) copy-start(pred[384,384]{1,0:T(8,128)(4,1)} %iota_compare_fusion) | copy-start | bytes 442372
  29.5 4.3 %copy-start.11 = (f32[32,384]{1,0:T(8,128)S(1)}, f32[32,384]{1,0:T(8,128)}, u32[]{:S(2)}) copy-start(f32[32,384]{1,0:T(8,128)} %get-tuple-element.168) | copy-start | bytes 147460
  29.5 4.3 %copy-start.12 = (f32[32,384]{1,0:T(8,128)S(1)}, f32[32,384]{1,0:T(8,128)}, u32[]{:S(2)}) copy-start(f32[32,384]{1,0:T(8,128)} %get-tuple-element.160) | copy-start | bytes 147460
  32.3 24.6 %collective-permute-start.2 = (bf16[32,64,128]{2,1,0:T(8,128)(2,1)S(1)}, bf16[32,64,128]{2,1,0:T(8,128)(2,1)S(1)}, u32[]{:S(2)}, u32[]{:S(2)}) collective-permute-start(bf16[32,64,128]{2,1,0:T(8,128)(2,1)S(1)} %fusion.43), channel_id=1, source_target_pairs={{0,4},{1,5},{2,6},{3,7},{8,12},{9,13},{10,14},{11,15},{16,20},{17,... | collective-permute-start | bytes 1572872 | tf_op jit(solution)/shard_map/while/body/eval_jaxpr/ppermute | solution.py:20
  56.9 1.5 %copy-start.1 = (bf16[1,384,2048]{1,2,0:T(8,128)(2,1)S(1)}, bf16[1,384,2048]{1,2,0:T(8,128)(2,1)}, u32[]{:S(2)}) copy-start(bf16[1,384,2048]{1,2,0:T(8,128)(2,1)} %copy.33) | copy-start | bytes 4718596
  56.9 1.5 %copy-start.6 = (f32[384,32]{0,1:T(8,128)S(1)}, f32[384,32]{0,1:T(8,128)}, u32[]{:S(2)}) copy-start(f32[384,32]{0,1:T(8,128)} %get-tuple-element.162) | copy-start | bytes 147460
  56.9 1.5 %copy-start.13 = (f32[2048]{0:T(1024)S(1)}, f32[2048]{0:T(1024)}, u32[]{:S(2)}) copy-start(f32[2048]{0:T(1024)} %mul.282) | copy-start | bytes 24580
  58.4 2.2 %copy-start.15 = (f32[1,2048]{1,0:T(1,128)S(1)}, f32[1,2048]{1,0:T(1,128)}, u32[]{:S(2)}) copy-start(f32[1,2048]{1,0:T(1,128)} %param.25) | copy-start | bytes 24580
  60.6 3.6 %copy-start.3 = (f32[1,8,384]{2,1,0:T(8,128)S(1)}, f32[1,8,384]{2,1,0:T(8,128)}, u32[]{:S(2)}) copy-start(f32[1,8,384]{2,1,0:T(8,128)} %custom-call.1) | copy-start | bytes 36868
  60.6 3.6 %copy-start.5 = (bf16[1,768,128]{2,1,0:T(8,128)(2,1)S(1)}, bf16[1,768,128]{2,1,0:T(8,128)(2,1)}, u32[]{:S(2)}) copy-start(bf16[1,768,128]{2,1,0:T(8,128)(2,1)} %all-gather.1) | copy-start | bytes 589828
  62.2 53.6 %collective-permute-start.3 = (bf16[384,2048]{0,1:T(8,128)(2,1)}, bf16[384,2048]{0,1:T(8,128)(2,1)S(1)}, u32[]{:S(2)}, u32[]{:S(2)}) collective-permute-start(bf16[384,2048]{0,1:T(8,128)(2,1)} %multiply_convert_fusion), channel_id=1, source_target_pairs={{0,8},{8,16},{16,24},{24,0},{1,9},{9,17},{17,25},{25,1},{2,10},{10... | collective-permute-start | bytes 4718600 | tf_op jit(solution)/shard_map/ppermute | solution.py:26
  68.8 5.3 %copy-start = (f32[384,384,8]{1,0,2:T(8,128)S(1)}, f32[384,384,8]{1,0,2:T(8,128)}, u32[]{:S(2)}) copy-start(f32[384,384,8]{1,0,2:T(8,128)} %get-tuple-element.250) | copy-start | bytes 14155780 | tf_op jit(solution)/shard_map/while
  79.8 5.8 %copy-start = (f32[384,384,8]{1,0,2:T(8,128)S(1)}, f32[384,384,8]{1,0,2:T(8,128)}, u32[]{:S(2)}) copy-start(f32[384,384,8]{1,0,2:T(8,128)} %get-tuple-element.250) | copy-start | bytes 14155780 | tf_op jit(solution)/shard_map/while
  89.4 26.5 %collective-permute-start.4 = (bf16[384,1024]{1,0:T(8,128)(2,1)S(1)}, bf16[384,1024]{1,0:T(8,128)(2,1)S(1)}, u32[]{:S(2)}, u32[]{:S(2)}) collective-permute-start(bf16[384,1024]{1,0:T(8,128)(2,1)S(1)} %bitcast.200), channel_id=1, source_target_pairs={{0,8},{8,16},{16,24},{24,0},{1,9},{9,17},{17,25},{25,1},{2,10},{10... | collective-permute-start | bytes 2359304 | tf_op jit(solution)/shard_map/ppermute | solution.py:26
where the time goes:
time: 120 us; the launch traced here: 118 us
  matrix products  45 us (38%)
  waiting for transfers between devices  25.2 us (21%)
  other arithmetic  18.3 us (15%)
  local copies, waits for them, and re-layouts  13.9 us (12%)
  starting transfers between devices  7.33 us (6%)
  blocking collectives  6.14 us (5%)
  loops' own time  1.41 us (1%)
    ppermute x2, waiting for transfers between devices, shifted_2(): return lax.ppermute(value, axis, pairs)  25.2 us
    dot_general x1, matrix products, local_scan(): jnp.einsum('ghts,sghp->tghp', weights, x_block.reshape(length, groups, pe...  23.1 us
    dot_general x2, matrix products, attend_block(): jnp.einsum('ljnx,xlc->ljnc', weights_exp.astype(jnp.bfloat16), value_grid...  11 us
    unnamed x50, local copies, waits for them, and re-layouts  8.14 us
    dot_general x2, matrix products, attend_block(): jnp.einsum('hbau,zbu->bahz', query_tile_layout, key_tile_layout, preferre...  6.03 us
    mul x1, other arithmetic, local_scan(): x_block * tail_decay[:, :, None]  5.15 us
    all_gather x1, blocking collectives, local(): lax.all_gather(key_local, 'ctx', axis=0, tiled=True)  4.07 us
    ppermute x3, starting transfers between devices, shifted(): return lax.ppermute(value, axis, pairs)  4.03 us
  transfers between devices with their start and end apart: 5, of which 1 were waited for; matrix products, arithmetic and copies ran while one was open for 49% of the time, Pallas kernels for 0%

commit v1 on v0

v1 whole, which is shorter than its diff:
```python
import functools
import math

import jax
import jax.numpy as jnp
from jax import lax
from jax.experimental import pallas as pl
from jax.experimental.pallas import tpu as pltpu
from jax.sharding import PartitionSpec as P

HDIM = 64
STATE = 128
KERNEL = 4
ADIM = 128
HALO = 16
LANES = 256
ROWS = 128
MESH = pl.DeviceIdType.MESH
highest = lax.Precision.HIGHEST


def silu(v):
    return v / (1.0 + jnp.exp(-v))


def split2(v):
    high = v.astype(jnp.bfloat16)
    return high, (v - high.astype(jnp.float32)).astype(jnp.bfloat16)


def split3(v):
    high = v.astype(jnp.bfloat16)
    rest = v - high.astype(jnp.float32)
    mid = rest.astype(jnp.bfloat16)
    low = (rest - mid.astype(jnp.float32)).astype(jnp.bfloat16)
    return jnp.concatenate([high, mid, low], axis=1)


def mm(a, b):
    return jnp.dot(a, b, preferred_element_type=jnp.float32)


def nt(a, b, precision=None):
    return lax.dot_general(
        a, b, (((1,), (1,)), ((), ())), precision=precision, preferred_element_type=jnp.float32
    )


def kernel(
    n_ctx,
    n_pipe,
    x_ref,
    bc_ref,
    z_ref,
    step_ref,
    bias_ref,
    rate_ref,
    skip_ref,
    cw_ref,
    cbw_ref,
    gain_ref,
    q_ref,
    k_ref,
    v_ref,
    doc_ref,
    mix_out,
    attn_out,
    kv_scr,
    halo_x,
    halo_bc,
    state_in,
    state_out,
    attn_scr,
    mix_scr,
    doc_scr,
    mask_scr,
    expand,
    x_ext,
    bc_ext,
    xc_scr,
    xt_hi,
    xt_lo,
    g_hi,
    g_lo,
    state_acc,
    gated,
    acc_scr,
    ml_scr,
    kv_send,
    kv_recv,
    halo_send,
    halo_recv,
    st_send,
    st_recv,
    at_send,
    at_recv,
    mx_send,
    mx_recv,
):
    me = lax.axis_index("ctx")
    stage = lax.axis_index("pipe")
    following = lax.rem(stage + 1, n_pipe)
    previous = lax.rem(stage + n_pipe - 1, n_pipe)
    rows, width = x_ref.shape
    heads = q_ref.shape[1] // ADIM
    blocks = rows // ROWS

    barrier = pltpu.get_barrier_semaphore()
    pl.semaphore_signal(barrier, inc=1, device_id={"pipe": following}, device_id_type=MESH)
    pl.semaphore_signal(barrier, inc=1, device_id={"pipe": previous}, device_id_type=MESH)
    for d in range(1, n_ctx):
        pl.semaphore_signal(
            barrier, inc=1, device_id={"ctx": lax.rem(me + d, n_ctx)}, device_id_type=MESH
        )
    pl.semaphore_wait(barrier, n_ctx + 1)

    def kv_copy(d, which):
        return pltpu.make_async_remote_copy(
            src_ref=(k_ref, v_ref)[which],
            dst_ref=kv_scr.at[which, d - 1],
            send_sem=kv_send.at[which, d - 1],
            recv_sem=kv_recv.at[which, d - 1],
            device_id={"ctx": lax.rem(me + d, n_ctx)},
            device_id_type=MESH,
        )

    def halo_copy(which):
        src, dst = ((x_ref, halo_x), (bc_ref, halo_bc))[which]
        return pltpu.make_async_remote_copy(
            src_ref=src.at[rows - HALO : rows],
            dst_ref=dst,
            send_sem=halo_send.at[which],
            recv_sem=halo_recv.at[which],
            device_id={"ctx": lax.rem(me + 1, n_ctx)},
            device_id_type=MESH,
        )

    def state_copy():
        return pltpu.make_async_remote_copy(
            src_ref=state_out,
            dst_ref=state_in,
            send_sem=st_send,
            recv_sem=st_recv,
            device_id={"ctx": lax.rem(me + 1, n_ctx)},
            device_id_type=MESH,
        )

    def attn_copy(h):
        columns = pl.ds(pl.multiple_of(h * ADIM, ADIM), ADIM)
        return pltpu.make_async_remote_copy(
            src_ref=attn_scr.at[h],
            dst_ref=attn_out.at[0, :, columns],
            send_sem=at_send.at[h],
            recv_sem=at_recv.at[h],
            device_id={"pipe": following},
            device_id_type=MESH,
        )

    def mix_copy(r):
        part = pl.ds(r * ROWS, ROWS)
        return pltpu.make_async_remote_copy(
            src_ref=mix_scr.at[part],
            dst_ref=mix_out.at[0, part],
            send_sem=mx_send.at[r],
            recv_sem=mx_recv.at[r],
            device_id={"pipe": following},
            device_id_type=MESH,
        )

    for d in range(1, n_ctx):

        @pl.when(me + d < n_ctx)
        def _():
            kv_copy(d, 0).start()
            kv_copy(d, 1).start()

    for which in range(2):
        halo_copy(which).start()

    row = lax.broadcasted_iota(jnp.int32, (rows, rows), 0)
    col = lax.broadcasted_iota(jnp.int32, (rows, rows), 1)

    def doc_row(shard):
        columns = pl.ds(pl.multiple_of(shard * rows, 128), rows)
        return doc_ref[:, columns].astype(jnp.float32)

    own_docs = jnp.broadcast_to(doc_row(me), (rows, rows))
    doc_scr[...] = own_docs.T
    mask_scr[...] = jnp.where((row >= col) & (own_docs == doc_scr[...]), 0.0, -1e30)

    for d in range(1, n_ctx):

        @pl.when(me - d >= 0)
        def _():
            kv_copy(d, 0).wait_recv()
            kv_copy(d, 1).wait_recv()

    scale = 1.0 / math.sqrt(ADIM)

    def one_head(h, carry):
        columns = pl.ds(pl.multiple_of(h * ADIM, ADIM), ADIM)
        query = q_ref[:, columns]
        logits = nt(query, k_ref[...]) * scale + mask_scr[...]
        top = jnp.max(logits, axis=1, keepdims=True)
        probs = jnp.exp(logits - top)
        ml_scr[0] = top
        ml_scr[1] = jnp.sum(probs, axis=1, keepdims=True)
        acc_scr[...] = mm(probs.astype(jnp.bfloat16), v_ref[...])
        for d in range(1, n_ctx):

            @pl.when(me - d >= 0)
            def _():
                shard = lax.rem(me - d + n_ctx, n_ctx)
                logits = nt(query, kv_scr[0, d - 1]) * scale
                logits = jnp.where(doc_row(shard) == doc_scr[...], logits, -1e30)
                old = ml_scr[0]
                top = jnp.maximum(old, jnp.max(logits, axis=1, keepdims=True))
                probs = jnp.exp(logits - top)
                fade = jnp.exp(old - top)
                ml_scr[0] = top
                ml_scr[1] = ml_scr[1] * fade + jnp.sum(probs, axis=1, keepdims=True)
                acc_scr[...] = acc_scr[...] * fade + mm(
                    probs.astype(jnp.bfloat16), kv_scr[1, d - 1]
                )

        attn_scr[h] = (acc_scr[...] / ml_scr[1]).astype(jnp.bfloat16)
        attn_copy(h).start()
        return carry

    lax.fori_loop(0, heads, one_head, 0)

    count = step_ref.shape[1]
    e_row = lax.rem(lax.broadcasted_iota(jnp.int32, (3 * count, width), 0), count)
    e_col = lax.broadcasted_iota(jnp.int32, (3 * count, width), 1) // HDIM
    expand[...] = jnp.where(e_row == e_col, 1.0, 0.0).astype(jnp.bfloat16)

    for which in range(2):
        halo_copy(which).wait_recv()
    keep = jnp.where(me > 0, 1.0, 0.0)
    x_ext[0:8] = halo_x[...].astype(jnp.float32)[HALO - 8 :] * keep
    x_ext[8 : 8 + rows] = x_ref[...].astype(jnp.float32)
    bc_ext[0:8] = halo_bc[...].astype(jnp.float32)[HALO - 8 :] * keep
    bc_ext[8 : 8 + rows] = bc_ref[...].astype(jnp.float32)
    first = 8 - (KERNEL - 1)

    def bc_conv(which):
        lanes = slice(which * STATE, (which + 1) * STATE)
        total = jnp.zeros((rows, STATE), jnp.float32)
        for tap in range(KERNEL):
            total = total + cbw_ref[tap, which : which + 1] * bc_ext[first + tap : first + tap + rows, lanes]
        return silu(total)

    b_conv = bc_conv(0)
    c_conv = bc_conv(1)
    gram = jnp.where(row >= col, nt(c_conv, b_conv, highest), 0.0)
    high, low = split2(gram)
    g_hi[...] = high
    g_lo[...] = low
    bt_hi, bt_lo = split2(b_conv.T)
    c_hi, c_lo = split2(c_conv)

    raw = step_ref[...].astype(jnp.float32) + bias_ref[...]
    step = jnp.maximum(raw, 0.0) + jnp.log1p(jnp.exp(-jnp.abs(raw)))
    log_decay = -rate_ref[...] * step
    lower = jnp.where(row >= col, 1.0, 0.0)
    cumulative = jnp.dot(lower, log_decay, precision=highest, preferred_element_type=jnp.float32)
    grow = split3(jnp.exp(-cumulative) * step)
    fall = split3(jnp.exp(cumulative))
    skip = split3(jnp.broadcast_to(skip_ref[...], (8, count)))

    def prepare(j, carry):
        lanes = pl.ds(pl.multiple_of(j * LANES, LANES), LANES)
        total = cw_ref[0:1, lanes] * x_ext[first : first + rows, lanes]
        for tap in range(1, KERNEL):
            total = total + cw_ref[tap : tap + 1, lanes] * x_ext[first + tap : first + tap + rows, lanes]
        conv = silu(total)
        xc_scr[:, lanes] = conv
        high, low = split2(conv * mm(grow, expand[:, lanes]))
        xt_hi[:, lanes] = high
        xt_lo[:, lanes] = low
        state_acc[:, lanes] = mm(bt_hi, high) + mm(bt_hi, low) + mm(bt_lo, high)
        return carry

    lax.fori_loop(0, width // LANES, prepare, 0)

    @pl.when(me == 0)
    def _():
        state_in[...] = jnp.zeros_like(state_in)

    if n_ctx > 1:

        @pl.when(me > 0)
        def _():
            state_copy().wait_recv()

        @pl.when(me < n_ctx - 1)
        def _():
            end = mm(fall[rows - 16 :], expand[...])[15:16]
            state_out[...] = (end * (state_in[...].astype(jnp.float32) + state_acc[...])).astype(
                jnp.bfloat16
            )
            state_copy().start()

    for r in range(blocks):
        part = slice(r * ROWS, (r + 1) * ROWS)
        upto = (r + 1) * ROWS

        def mix_lanes(j, square):
            lanes = pl.ds(pl.multiple_of(j * LANES, LANES), LANES)
            inside = mm(g_hi[part, :upto], xt_hi[:upto, lanes])
            inside = inside + mm(g_hi[part, :upto], xt_lo[:upto, lanes])
            inside = inside + mm(g_lo[part, :upto], xt_hi[:upto, lanes])
            carried = state_in[:, lanes]
            inside = inside + mm(c_hi[part], carried) + mm(c_lo[part], carried)
            e_part = expand[:, lanes]
            out = inside * mm(fall[part], e_part) + mm(skip, e_part)[0:1] * xc_scr[part, lanes]
            out = out * silu(z_ref[part, lanes].astype(jnp.float32))
            gated[:, lanes] = out
            return square + jnp.sum(out * out, axis=1, keepdims=True)

        square = lax.fori_loop(0, width // LANES, mix_lanes, jnp.zeros((ROWS, 1), jnp.float32))
        norm = lax.rsqrt(square * (1.0 / width) + 1e-05)
        mix_scr[part] = (gated[...] * norm * gain_ref[...]).astype(jnp.bfloat16)
        mix_copy(r).start()

    for d in range(1, n_ctx):

        @pl.when(me + d < n_ctx)
        def _():
            kv_copy(d, 0).wait_send()
            kv_copy(d, 1).wait_send()

    for which in range(2):
        halo_copy(which).wait_send()
    if n_ctx > 1:

        @pl.when(me < n_ctx - 1)
        def _():
            state_copy().wait_send()

    def finish(h, carry):
        attn_copy(h).wait()
        return carry

    lax.fori_loop(0, heads, finish, 0)
    for r in range(blocks):
        mix_copy(r).wait()


def local(
    mamba_input,
    mamba_bc,
    gate_input,
    step_input,
    step_bias,
    decay_rate,
    skip_gain,
    conv_weight,
    conv_bc_weight,
    norm_gain,
    queries,
    attn_keys,
    attn_values,
    documents,
):
    n_ctx = lax.axis_size("ctx")
    n_pipe = lax.axis_size("pipe")
    _, rows, width = mamba_input.shape
    q_width = queries.shape[2]
    heads = q_width // ADIM
    count = step_input.shape[2]
    bf16, f32 = jnp.bfloat16, jnp.float32
    others = max(n_ctx - 1, 1)
    dma = pltpu.SemaphoreType.DMA
    vmem = pl.BlockSpec(memory_space=pltpu.VMEM)
    mixer, attended = pl.pallas_call(
        functools.partial(kernel, n_ctx, n_pipe),
        out_shape=(
            jax.ShapeDtypeStruct(mamba_input.shape, bf16),
            jax.ShapeDtypeStruct(queries.shape, bf16),
        ),
        in_specs=[vmem] * 14,
        out_specs=[pl.BlockSpec(memory_space=pl.ANY)] * 2,
        scratch_shapes=[
            pltpu.VMEM((2, others, rows, ADIM), bf16),
            pltpu.VMEM((HALO, width), bf16),
            pltpu.VMEM((HALO, 2 * STATE), bf16),
            pltpu.VMEM((STATE, width), bf16),
            pltpu.VMEM((STATE, width), bf16),
            pltpu.VMEM((heads, rows, ADIM), bf16),
            pltpu.VMEM((rows, width), bf16),
            pltpu.VMEM((rows, rows), f32),
            pltpu.VMEM((rows, rows), f32),
            pltpu.VMEM((3 * count, width), bf16),
            pltpu.VMEM((rows + 8, width), f32),
            pltpu.VMEM((rows + 8, 2 * STATE), f32),
            pltpu.VMEM((rows, width), f32),
            pltpu.VMEM((rows, width), bf16),
            pltpu.VMEM((rows, width), bf16),
            pltpu.VMEM((rows, rows), bf16),
            pltpu.VMEM((rows, rows), bf16),
            pltpu.VMEM((STATE, width), f32),
            pltpu.VMEM((ROWS, width), f32),
            pltpu.VMEM((rows, ADIM), f32),
            pltpu.VMEM((2, rows, 1), f32),
            dma((2, others)),
            dma((2, others)),
            dma((2,)),
            dma((2,)),
            dma,
            dma,
            dma((heads,)),
            dma((heads,)),
            dma((rows // ROWS,)),
            dma((rows // ROWS,)),
        ],
        compiler_params=pltpu.CompilerParams(
            collective_id=0, has_side_effects=True, vmem_limit_bytes=48 * 1024 * 1024
        ),
    )(
        mamba_input[0],
        mamba_bc[0].reshape(rows, 2 * STATE),
        gate_input[0],
        step_input[0],
        step_bias,
        decay_rate,
        skip_gain,
        conv_weight[0],
        conv_bc_weight[0],
        norm_gain,
        queries[0],
        attn_keys[0],
        attn_values[0],
        documents,
    )
    return mixer, attended


def solution(mesh):
    in_specs = (
        P("pipe", "ctx", "tp"),
        P("pipe", "ctx", None, "tp"),
        P("pipe", "ctx", "tp"),
        P("pipe", "ctx", "tp"),
        P("pipe", "tp"),
        P("pipe", "tp"),
        P("pipe", "tp"),
        P("pipe", None, "tp"),
        P("pipe", None, None, "tp"),
        P("pipe", "tp"),
        P("pipe", "ctx", "tp"),
        P("pipe", "ctx", "tp"),
        P("pipe", "ctx", "tp"),
        P("pipe", None),
    )
    out_specs = (P("pipe", "ctx", "tp"), P("pipe", "ctx", "tp"))
    return jax.shard_map(local, mesh=mesh, in_specs=in_specs, out_specs=out_specs, check_vma=False)
```

time: 120 us -> 72.5 us (0.60)
  Pallas kernels: 0 us -> 58.4 us
  matrix products: 45 us -> 0 us
  waiting for transfers between devices: 25.2 us -> 0 us
  other arithmetic: 18.3 us -> 0 us
  starting transfers between devices: 7.33 us -> 0 us
  blocking collectives: 6.14 us -> 0 us
  loops' own time: 1.41 us -> 0 us
    pallas_call x0 -> x1, Pallas kernels: none -> 58.4 us  [local(): pl.pallas_call(functools.partial(kernel, n_ctx, n_pipe), out_shape=(jax.S...]
    dot_general x8 -> x0, matrix products: 45 us -> none  [the longest x1 23.1 us: local_scan(): jnp.einsum('ghts,sghp->tghp', weights, x_block.reshape(length, groups, pe...]
    ppermute x5 -> x0, waiting for transfers between devices: 25.2 us -> none  [the longest x2 25.2 us: shifted_2(): return lax.ppermute(value, axis, pairs)]
    ppermute x5 -> x0, starting transfers between devices: 7.33 us -> none  [the longest x3 4.03 us: shifted(): return lax.ppermute(value, axis, pairs)]
    mul x6 -> x0, other arithmetic: 6.77 us -> none  [the longest x1 5.15 us: local_scan(): x_block * tail_decay[:, :, None]]
    all_gather x2 -> x0, blocking collectives: 6.14 us -> none  [the longest x1 4.07 us: local(): lax.all_gather(key_local, 'ctx', axis=0, tiled=True)]
    unnamed x50 -> x26, local copies, waits for them, and re-layouts: 8.14 us -> 12.9 us
    reduce_sum x3 -> x0, other arithmetic: 4.44 us -> none  [the longest x2 2.29 us: attend_block(): new_total = row_sum_running * rescale + jnp.sum(weights_exp, axis=-1)]
  transfers between devices with their start and end apart: 5 -> 0, of which waited for: 1 -> 0; matrix products, arithmetic and copies ran while one was open for 49% -> 0% of each run, Pallas kernels for 0% -> 0%
where the time goes in v1:
time: 72.5 us; the launch traced here: 72 us
  Pallas kernels  58.4 us (81%)
  local copies, waits for them, and re-layouts  12.9 us (18%)
    pallas_call x1, Pallas kernels, local(): pl.pallas_call(functools.partial(kernel, n_ctx, n_pipe), out_shape=(jax.S...  58.4 us
    unnamed x26, local copies, waits for them, and re-layouts  12.9 us

profile of v1, /device:TPU:1, one launch (start us, length us, event | category | flops | bytes accessed | tf_op | source)
XLA Modules:
  0.0 72.0 jit_solution(18017385602939355252)
XLA Ops:
  0.6 0.9 %copy.16 = bf16[1,384,32]{2,1,0:T(8,128)(2,1)S(1)} copy(bf16[1,384,32]{1,2,0:T(8,128)(2,1)} %param.17) | data formatting | bytes 49152 | tf_op args[3]
  1.5 1.0 %copy.19 = bf16[48,8,2,128]{3,1,2,0:T(8,128)(2,1)S(1)} copy(bf16[48,8,2,128]{3,2,1,0:T(2,128)(2,1)} %bitcast.22) | data formatting | bytes 393216
  2.4 0.0 copy-start
  2.5 1.4 %copy-done = bf16[1,384,2048]{2,1,0:T(8,128)(2,1)S(1)} copy-done((bf16[1,384,2048]{2,1,0:T(8,128)(2,1)S(1)}, bf16[1,384,2048]{2,1,0:T(8,128)(2,1)}, u32[]{:S(2)}) %copy-start) | copy-done | bytes 1572888
  3.9 0.0 copy-start.1
  3.9 1.1 %copy-done.1 = bf16[1,384,1024]{2,1,0:T(8,128)(2,1)S(1)} copy-done((bf16[1,384,1024]{2,1,0:T(8,128)(2,1)S(1)}, bf16[1,384,1024]{2,1,0:T(8,128)(2,1)}, u32[]{:S(2)}) %copy-start.1) | copy-done | bytes 786456
  5.0 0.0 copy-start.2
  5.0 0.9 %copy-done.2 = bf16[1,384,128]{2,1,0:T(8,128)(2,1)S(1)} copy-done((bf16[1,384,128]{2,1,0:T(8,128)(2,1)S(1)}, bf16[1,384,128]{2,1,0:T(8,128)(2,1)}, u32[]{:S(2)}) %copy-start.2) | copy-done | bytes 98328
  5.9 0.0 copy-start.3
  5.9 0.9 %copy-done.3 = bf16[1,384,128]{2,1,0:T(8,128)(2,1)S(1)} copy-done((bf16[1,384,128]{2,1,0:T(8,128)(2,1)S(1)}, bf16[1,384,128]{2,1,0:T(8,128)(2,1)}, u32[]{:S(2)}) %copy-start.3) | copy-done | bytes 98328
  6.8 0.0 copy-start.4
  6.8 0.8 %copy-done.4 = f32[1,4,2048]{2,1,0:T(4,128)S(1)} copy-done((f32[1,4,2048]{2,1,0:T(4,128)S(1)}, f32[1,4,2048]{2,1,0:T(4,128)}, u32[]{:S(2)}) %copy-start.4) | copy-done | bytes 32792
  7.5 0.0 copy-start.5
  7.5 0.7 copy-done.5
  8.2 0.0 copy-start.6
  8.2 0.7 copy-done.6
  8.9 0.0 copy-start.7
  8.9 0.7 copy-done.7
  9.6 0.0 copy-start.8
  9.6 0.7 copy-done.8
  10.3 0.0 copy-start.9
  10.3 0.7 copy-done.9
  10.9 0.0 copy-start.10
  10.9 0.7 copy-done.10
  11.6 58.4 %shard_map.149 = (bf16[1,384,2048]{2,1,0:T(8,128)(2,1)S(1)}, bf16[1,384,1024]{2,1,0:T(8,128)(2,1)S(1)}) custom-call(bf16[384,2048]{1,0:T(8,128)(2,1)S(1)} %bitcast.13, bf16[384,256]{1,0:T(8,128)(2,1)S(1)} %bitcast.14, bf16[384,2048]{1,0:T(8,128)(2,1)} %bitcast.21, bf16[384,32]{1,0:T(8,128)(2,1)S(1)} %bitcast.16, f32[1,32]{1,0:T(1,128)S(1)} %copy-done.8, ...), custom_call_target="tpu_custom_call" | custom-call | tf_op jit(solution)/shard_map/pallas_call | solution.py:376
  69.9 1.1 %copy.22 = bf16[1,384,2048]{2,1,0:T(8,128)(2,1)} copy(bf16[1,384,2048]{2,1,0:T(8,128)(2,1)S(1)} %get-tuple-element.4) | data formatting | bytes 3145728
  71.1 0.9 %copy.23 = bf16[1,384,1024]{2,1,0:T(8,128)(2,1)} copy(bf16[1,384,1024]{2,1,0:T(8,128)(2,1)S(1)} %get-tuple-element.5) | data formatting | bytes 1572864
Async XLA Ops:
  2.4 1.4 %copy-start = (bf16[1,384,2048]{2,1,0:T(8,128)(2,1)S(1)}, bf16[1,384,2048]{2,1,0:T(8,128)(2,1)}, u32[]{:S(2)}) copy-start(bf16[1,384,2048]{2,1,0:T(8,128)(2,1)} %param.14) | copy-start | bytes 4718596
  3.9 1.1 %copy-start.1 = (bf16[1,384,1024]{2,1,0:T(8,128)(2,1)S(1)}, bf16[1,384,1024]{2,1,0:T(8,128)(2,1)}, u32[]{:S(2)}) copy-start(bf16[1,384,1024]{2,1,0:T(8,128)(2,1)} %param.24) | copy-start | bytes 2359300
  5.0 0.9 %copy-start.2 = (bf16[1,384,128]{2,1,0:T(8,128)(2,1)S(1)}, bf16[1,384,128]{2,1,0:T(8,128)(2,1)}, u32[]{:S(2)}) copy-start(bf16[1,384,128]{2,1,0:T(8,128)(2,1)} %param.25) | copy-start | bytes 294916
  5.9 0.9 %copy-start.3 = (bf16[1,384,128]{2,1,0:T(8,128)(2,1)S(1)}, bf16[1,384,128]{2,1,0:T(8,128)(2,1)}, u32[]{:S(2)}) copy-start(bf16[1,384,128]{2,1,0:T(8,128)(2,1)} %param.26) | copy-start | bytes 294916
  6.8 0.8 %copy-start.4 = (f32[1,4,2048]{2,1,0:T(4,128)S(1)}, f32[1,4,2048]{2,1,0:T(4,128)}, u32[]{:S(2)}) copy-start(f32[1,4,2048]{2,1,0:T(4,128)} %param.21) | copy-start | bytes 98308
  7.5 0.7 copy-start.5
  8.2 0.7 copy-start.6
  8.9 0.7 copy-start.7
  9.6 0.7 copy-start.8
  10.3 0.7 copy-start.9
  10.9 0.7 copy-start.10

commit v2 on v1

--- a/solution.py
+++ b/solution.py
@@ -49,6 +49,22 @@
 def kernel(
     n_ctx,
     n_pipe,
+    x_hbm,
+    bc_hbm,
+    z_hbm,
+    step_hbm,
+    bias_hbm,
+    rate_hbm,
+    skip_hbm,
+    cw_hbm,
+    cbw_hbm,
+    gain_hbm,
+    q_hbm,
+    k_hbm,
+    v_hbm,
+    doc_hbm,
+    mix_out,
+    attn_out,
     x_ref,
     bc_ref,
     z_ref,
@@ -63,8 +79,7 @@
     k_ref,
     v_ref,
     doc_ref,
-    mix_out,
-    attn_out,
+    load_sem,
     kv_scr,
     halo_x,
     halo_bc,
@@ -105,6 +120,17 @@
     heads = q_ref.shape[1] // ADIM
     blocks = rows // ROWS
 
+    sources = (x_hbm, bc_hbm, z_hbm, step_hbm, bias_hbm, rate_hbm, skip_hbm)
+    sources += (cw_hbm, cbw_hbm, gain_hbm, q_hbm, k_hbm, v_hbm, doc_hbm)
+    targets = (x_ref, bc_ref, z_ref, step_ref, bias_ref, rate_ref, skip_ref)
+    targets += (cw_ref, cbw_ref, gain_ref, q_ref, k_ref, v_ref, doc_ref)
+    loads = [
+        pltpu.make_async_copy(source, target, load_sem.at[i])
+        for i, (source, target) in enumerate(zip(sources, targets))
+    ]
+    for i in (13, 11, 12, 10, 0, 1, 3, 4, 5, 6, 7, 8, 9, 2):
+        loads[i].start()
+
     barrier = pltpu.get_barrier_semaphore()
     pl.semaphore_signal(barrier, inc=1, device_id={"pipe": following}, device_id_type=MESH)
     pl.semaphore_signal(barrier, inc=1, device_id={"pipe": previous}, device_id_type=MESH)
@@ -112,11 +138,9 @@
         pl.semaphore_signal(
             barrier, inc=1, device_id={"ctx": lax.rem(me + d, n_ctx)}, device_id_type=MESH
         )
-    pl.semaphore_wait(barrier, n_ctx + 1)
-
     def kv_copy(d, which):
         return pltpu.make_async_remote_copy(
-            src_ref=(k_ref, v_ref)[which],
+            src_ref=(k_hbm, v_hbm)[which],
             dst_ref=kv_scr.at[which, d - 1],
             send_sem=kv_send.at[which, d - 1],
             recv_sem=kv_recv.at[which, d - 1],
@@ -125,9 +149,9 @@
         )
 
     def halo_copy(which):
-        src, dst = ((x_ref, halo_x), (bc_ref, halo_bc))[which]
+        src, dst = ((x_hbm, halo_x), (bc_hbm, halo_bc))[which]
         return pltpu.make_async_remote_copy(
-            src_ref=src.at[rows - HALO : rows],
+            src_ref=src.at[src.shape[0] - dst.shape[0] : src.shape[0]],
             dst_ref=dst,
             send_sem=halo_send.at[which],
             recv_sem=halo_recv.at[which],
@@ -167,16 +191,6 @@
             device_id_type=MESH,
         )
 
-    for d in range(1, n_ctx):
-
-        @pl.when(me + d < n_ctx)
-        def _():
-            kv_copy(d, 0).start()
-            kv_copy(d, 1).start()
-
-    for which in range(2):
-        halo_copy(which).start()
-
     row = lax.broadcasted_iota(jnp.int32, (rows, rows), 0)
     col = lax.broadcasted_iota(jnp.int32, (rows, rows), 1)
 
@@ -184,9 +198,25 @@
         columns = pl.ds(pl.multiple_of(shard * rows, 128), rows)
         return doc_ref[:, columns].astype(jnp.float32)
 
+    pl.semaphore_wait(barrier, n_ctx + 1)
+
+    for d in range(1, n_ctx):
+
+        @pl.when(me + d < n_ctx)
+        def _():
+            kv_copy(d, 0).start()
+            kv_copy(d, 1).start()
+
+    for which in range(2):
+        halo_copy(which).start()
+
+    loads[13].wait()
     own_docs = jnp.broadcast_to(doc_row(me), (rows, rows))
     doc_scr[...] = own_docs.T
     mask_scr[...] = jnp.where((row >= col) & (own_docs == doc_scr[...]), 0.0, -1e30)
+
+    for i in (11, 12, 10):
+        loads[i].wait()
 
     for d in range(1, n_ctx):
 
@@ -229,25 +259,27 @@
 
     lax.fori_loop(0, heads, one_head, 0)
 
-    count = step_ref.shape[1]
+    count = step_ref.shape[0]
     e_row = lax.rem(lax.broadcasted_iota(jnp.int32, (3 * count, width), 0), count)
     e_col = lax.broadcasted_iota(jnp.int32, (3 * count, width), 1) // HDIM
     expand[...] = jnp.where(e_row == e_col, 1.0, 0.0).astype(jnp.bfloat16)
 
+    for i in (0, 1, 3, 4, 5, 6, 7, 8):
+        loads[i].wait()
     for which in range(2):
         halo_copy(which).wait_recv()
     keep = jnp.where(me > 0, 1.0, 0.0)
     x_ext[0:8] = halo_x[...].astype(jnp.float32)[HALO - 8 :] * keep
     x_ext[8 : 8 + rows] = x_ref[...].astype(jnp.float32)
-    bc_ext[0:8] = halo_bc[...].astype(jnp.float32)[HALO - 8 :] * keep
-    bc_ext[8 : 8 + rows] = bc_ref[...].astype(jnp.float32)
+    bc_ext[0:16] = halo_bc[...].astype(jnp.float32)[2 * HALO - 16 :] * keep
+    bc_ext[16 : 16 + 2 * rows] = bc_ref[...].astype(jnp.float32)
     first = 8 - (KERNEL - 1)
 
     def bc_conv(which):
-        lanes = slice(which * STATE, (which + 1) * STATE)
         total = jnp.zeros((rows, STATE), jnp.float32)
         for tap in range(KERNEL):
-            total = total + cbw_ref[tap, which : which + 1] * bc_ext[first + tap : first + tap + rows, lanes]
+            tokens = bc_ext[pl.ds(2 * (first + tap) + which, rows, stride=2)]
+            total = total + cbw_ref[tap, which : which + 1] * tokens
         return silu(total)
 
     b_conv = bc_conv(0)
@@ -259,7 +291,7 @@
     bt_hi, bt_lo = split2(b_conv.T)
     c_hi, c_lo = split2(c_conv)
 
-    raw = step_ref[...].astype(jnp.float32) + bias_ref[...]
+    raw = step_ref[...].astype(jnp.float32).T + bias_ref[...]
     step = jnp.maximum(raw, 0.0) + jnp.log1p(jnp.exp(-jnp.abs(raw)))
     log_decay = -rate_ref[...] * step
     lower = jnp.where(row >= col, 1.0, 0.0)
@@ -301,6 +333,8 @@
             )
             state_copy().start()
 
+    loads[2].wait()
+    loads[9].wait()
     for r in range(blocks):
         part = slice(r * ROWS, (r + 1) * ROWS)
         upto = (r + 1) * ROWS
@@ -372,19 +406,36 @@
     bf16, f32 = jnp.bfloat16, jnp.float32
     others = max(n_ctx - 1, 1)
     dma = pltpu.SemaphoreType.DMA
-    vmem = pl.BlockSpec(memory_space=pltpu.VMEM)
+    operands = (
+        mamba_input[0],
+        mamba_bc[0].reshape(2 * rows, STATE),
+        gate_input[0],
+        step_input[0].T,
+        step_bias,
+        decay_rate,
+        skip_gain,
+        conv_weight[0],
+        conv_bc_weight[0],
+        norm_gain,
+        queries[0],
+        attn_keys[0],
+        attn_values[0],
+        documents,
+    )
     mixer, attended = pl.pallas_call(
         functools.partial(kernel, n_ctx, n_pipe),
         out_shape=(
             jax.ShapeDtypeStruct(mamba_input.shape, bf16),
             jax.ShapeDtypeStruct(queries.shape, bf16),
         ),
-        in_specs=[vmem] * 14,
+        in_specs=[pl.BlockSpec(memory_space=pltpu.HBM)] * len(operands),
         out_specs=[pl.BlockSpec(memory_space=pl.ANY)] * 2,
-        scratch_shapes=[
+        scratch_shapes=[pltpu.VMEM(operand.shape, operand.dtype) for operand in operands]
+        + [
+            dma((len(operands),)),
             pltpu.VMEM((2, others, rows, ADIM), bf16),
             pltpu.VMEM((HALO, width), bf16),
-            pltpu.VMEM((HALO, 2 * STATE), bf16),
+            pltpu.VMEM((2 * HALO, STATE), bf16),
             pltpu.VMEM((STATE, width), bf16),
             pltpu.VMEM((STATE, width), bf16),
             pltpu.VMEM((heads, rows, ADIM), bf16),
@@ -393,7 +444,7 @@
             pltpu.VMEM((rows, rows), f32),
             pltpu.VMEM((3 * count, width), bf16),
             pltpu.VMEM((rows + 8, width), f32),
-            pltpu.VMEM((rows + 8, 2 * STATE), f32),
+            pltpu.VMEM((2 * rows + 16, STATE), f32),
             pltpu.VMEM((rows, width), f32),
             pltpu.VMEM((rows, width), bf16),
             pltpu.VMEM((rows, width), bf16),
@@ -415,24 +466,9 @@
             dma((rows // ROWS,)),
         ],
         compiler_params=pltpu.CompilerParams(
-            collective_id=0, has_side_effects=True, vmem_limit_bytes=48 * 1024 * 1024
+            collective_id=0, has_side_effects=True, vmem_limit_bytes=62_000_000
         ),
-    )(
-        mamba_input[0],
-        mamba_bc[0].reshape(rows, 2 * STATE),
-        gate_input[0],
-        step_input[0],
-        step_bias,
-        decay_rate,
-        skip_gain,
-        conv_weight[0],
-        conv_bc_weight[0],
-        norm_gain,
-        queries[0],
-        attn_keys[0],
-        attn_values[0],
-        documents,
-    )
+    )(*operands)
     return mixer, attended
 
 

time: 72.5 us -> 62.3 us (0.86)
  local copies, waits for them, and re-layouts: 12.9 us -> 3.68 us
    unnamed x26 -> x4, local copies, waits for them, and re-layouts: 12.9 us -> 3.68 us
where the time goes in v2:
time: 62.3 us; the launch traced here: 62.1 us
  Pallas kernels  57.8 us (93%)
  local copies, waits for them, and re-layouts  3.68 us (6%)
  between operations  0.65 us (1%)
    pallas_call x1, Pallas kernels, local(): pl.pallas_call(functools.partial(kernel, n_ctx, n_pipe), out_shape=(jax.S...  57.8 us
    unnamed x4, local copies, waits for them, and re-layouts  3.68 us

profile of v2, /device:TPU:1, one launch (start us, length us, event | category | flops | bytes accessed | tf_op | source)
XLA Modules:
  0.0 62.1 jit_solution(5677748150116832159)
XLA Ops:
  0.6 57.8 %shard_map.149 = (bf16[1,384,2048]{2,1,0:T(8,128)(2,1)}, bf16[1,384,1024]{2,1,0:T(8,128)(2,1)}) custom-call(bf16[384,2048]{1,0:T(8,128)(2,1)} %bitcast.11, bf16[768,128]{1,0:T(8,128)(2,1)} %bitcast.14, bf16[384,2048]{1,0:T(8,128)(2,1)} %bitcast.12, bf16[32,384]{1,0:T(8,128)(2,1)} %bitcast.18, f32[1,32]{1,0:T(1,128)} %bias_hbm.1, f32[1,32]{1,0:T(1,128)} %rate_hbm.1, ...), custom_call_target="tpu_custom_call" | custom-call | tf_op jit(solution)/shard_map/pallas_call | solution.py:425
  58.4 0.0 copy-start
  58.4 2.8 %copy.18 = bf16[1,384,2048]{2,1,0:T(8,128)(2,1)} copy(bf16[1,384,2048]{2,1,0:T(8,128)(2,1)} %get-tuple-element.4) | data formatting | bytes 3145728
  61.2 0.0 copy-done
  61.2 0.9 %copy.19 = bf16[1,384,1024]{2,1,0:T(8,128)(2,1)} copy(bf16[1,384,1024]{2,1,0:T(8,128)(2,1)S(1)} %copy-done) | data formatting | bytes 1572864
Async XLA Ops:
  58.4 2.8 %copy-start = (bf16[1,384,1024]{2,1,0:T(8,128)(2,1)S(1)}, bf16[1,384,1024]{2,1,0:T(8,128)(2,1)}, u32[]{:S(2)}) copy-start(bf16[1,384,1024]{2,1,0:T(8,128)(2,1)} %get-tuple-element.5) | copy-start | bytes 2359300

commit v3 on v2

--- a/solution.py
+++ b/solution.py
@@ -198,6 +198,11 @@
         columns = pl.ds(pl.multiple_of(shard * rows, 128), rows)
         return doc_ref[:, columns].astype(jnp.float32)
 
+    loads[13].wait()
+    own_docs = jnp.broadcast_to(doc_row(me), (rows, rows))
+    doc_scr[...] = own_docs.T
+    mask_scr[...] = jnp.where((row >= col) & (own_docs == doc_scr[...]), 0.0, -1e30)
+
     pl.semaphore_wait(barrier, n_ctx + 1)
 
     for d in range(1, n_ctx):
@@ -209,11 +214,6 @@
 
     for which in range(2):
         halo_copy(which).start()
-
-    loads[13].wait()
-    own_docs = jnp.broadcast_to(doc_row(me), (rows, rows))
-    doc_scr[...] = own_docs.T
-    mask_scr[...] = jnp.where((row >= col) & (own_docs == doc_scr[...]), 0.0, -1e30)
 
     for i in (11, 12, 10):
         loads[i].wait()
@@ -379,6 +379,29 @@
     lax.fori_loop(0, heads, finish, 0)
     for r in range(blocks):
         mix_copy(r).wait()
+
+
+def store(mix_ref, attn_ref, mix_out, attn_out, mix_scr, attn_scr, load_sem, store_sem):
+    pieces = []
+    for source, stage, target in ((mix_ref, mix_scr, mix_out), (attn_ref, attn_scr, attn_out)):
+        for r in range(source.shape[1] // ROWS):
+            part = pl.ds(r * ROWS, ROWS)
+            pieces.append((source.at[:, part], stage.at[:, part], target.at[:, part]))
+    loads = [
+        pltpu.make_async_copy(source, stage, load_sem.at[i])
+        for i, (source, stage, _) in enumerate(pieces)
+    ]
+    stores = [
+        pltpu.make_async_copy(stage, target, store_sem.at[i])
+        for i, (_, stage, target) in enumerate(pieces)
+    ]
+    for load in loads:
+        load.start()
+    for load, put in zip(loads, stores):
+        load.wait()
+        put.start()
+    for put in stores:
+        put.wait()
 
 
 def local(
@@ -469,7 +492,22 @@
             collective_id=0, has_side_effects=True, vmem_limit_bytes=62_000_000
         ),
     )(*operands)
-    return mixer, attended
+    return pl.pallas_call(
+        store,
+        out_shape=(
+            jax.ShapeDtypeStruct(mamba_input.shape, bf16),
+            jax.ShapeDtypeStruct(queries.shape, bf16),
+        ),
+        in_specs=[pl.BlockSpec(memory_space=pl.ANY)] * 2,
+        out_specs=[pl.BlockSpec(memory_space=pl.ANY)] * 2,
+        scratch_shapes=[
+            pltpu.VMEM(mamba_input.shape, bf16),
+            pltpu.VMEM(queries.shape, bf16),
+            dma((2 * (rows // ROWS),)),
+            dma((2 * (rows // ROWS),)),
+        ],
+        compiler_params=pltpu.CompilerParams(vmem_limit_bytes=62_000_000),
+    )(mixer, attended)
 
 
 def solution(mesh):

time: 62.3 us -> 61.1 us (0.981)
  local copies, waits for them, and re-layouts: 3.68 us -> 0 us
  Pallas kernels: 57.8 us -> 60.3 us
    unnamed x4 -> x0, local copies, waits for them, and re-layouts: 3.68 us -> none
    pallas_call x0 -> x1, Pallas kernels: none -> 2.54 us  [local(): pl.pallas_call(store, out_shape=(jax.ShapeDtypeStruct(mamba_input.shape,...]
where the time goes in v3:
time: 61.1 us; the launch traced here: 60.9 us
  Pallas kernels  60.3 us (99%)
  between operations  0.64 us (1%)
    pallas_call x1, Pallas kernels, local(): pl.pallas_call(functools.partial(kernel, n_ctx, n_pipe), out_shape=(jax.S...  57.8 us
    pallas_call x1, Pallas kernels, local(): pl.pallas_call(store, out_shape=(jax.ShapeDtypeStruct(mamba_input.shape,...  2.54 us

profile of v3, /device:TPU:1, one launch (start us, length us, event | category | flops | bytes accessed | tf_op | source)
XLA Modules:
  0.0 60.9 jit_solution(9687503716067911745)
XLA Ops:
  0.6 57.8 %shard_map.149 = (bf16[1,384,2048]{2,1,0:T(8,128)(2,1)}, bf16[1,384,1024]{2,1,0:T(8,128)(2,1)}) custom-call(bf16[384,2048]{1,0:T(8,128)(2,1)} %bitcast.11, bf16[768,128]{1,0:T(8,128)(2,1)} %bitcast.14, bf16[384,2048]{1,0:T(8,128)(2,1)} %bitcast.12, bf16[32,384]{1,0:T(8,128)(2,1)} %bitcast.18, f32[1,32]{1,0:T(1,128)} %bias_hbm.1, f32[1,32]{1,0:T(1,128)} %rate_hbm.1, ...), custom_call_target="tpu_custom_call" | custom-call | tf_op jit(solution)/shard_map/pallas_call | solution.py:448
  58.4 2.5 %shard_map.150 = (bf16[1,384,2048]{2,1,0:T(8,128)(2,1)}, bf16[1,384,1024]{2,1,0:T(8,128)(2,1)}) custom-call(bf16[1,384,2048]{2,1,0:T(8,128)(2,1)} %get-tuple-element.4.mix_ref, bf16[1,384,1024]{2,1,0:T(8,128)(2,1)} %get-tuple-element.5.attn_ref), custom_call_target="tpu_custom_call" | custom-call | tf_op jit(solution)/shard_map/pallas_call | solution.py:495
